TPU v7x, 32 devices: a whole 2x2x4 slice. The times are simulated.
32 devices in a mesh: ka: 2 (over core), pair: 16 (over z, y, x).
Axes of the slice: x: 2, y: 2, z: 4, core: 2. Of those that a mesh axis runs over, the one named last changes fastest.
Arguments:
- cond_orbitals: bfloat16 [2, 2048, 2048], P('ka', 'pair'), may hold values from -6 to 6
- cond_energy: float32 [2, 2048], P('ka', 'pair'), may hold values from 0.5 to 8
- val_orbitals: bfloat16 [32, 2048], P(('ka', 'pair')), may hold values from -6 to 6
- val_energy: bfloat16 [32], P(('ka', 'pair')), may hold values from -8 to -0.5
- val_slots: int32 [2, 16, 16], P('ka', 'pair'), may hold values from 0 to 31
- owner_count: int32 [2, 16], P('ka', 'pair'), may hold values from 1 to 16, as said below
Outputs:
- response: float32 [2, 2048, 512], P('ka', 'pair')
Inputs may be any that keep to these rules, and one draw needn't show every extreme that they name: `owner_count`: in every lane some owner has exactly 16 live slots.
All inputs are finite; a program needn't handle non-finite values.
Results may differ from a plain program's by a relative error of at most 0.0047.
The roundings to bfloat16 on the way count: a program that leaves them out, or rounds other values in their place, can miss the bound.
Values may be sent and summed in bfloat16 or wider, within the bound.
A program may use at most 64 MiB of HBM per device.

v0:
```python
import jax
import jax.numpy as jnp
from jax import lax
from jax.sharding import PartitionSpec as P

BC = 128
GA = 16
GB = 128
WIN = 512
SLOTS = 16


def cosine_table(length):
    freq = lax.iota(jnp.float32, length)[:, None]
    point = lax.iota(jnp.float32, length)[None, :]
    factor = jnp.where(freq == 0, jnp.sqrt(1.0 / length), jnp.sqrt(2.0 / length))
    return (factor * jnp.cos(jnp.pi * (point + 0.5) * freq / length)).astype(jnp.bfloat16)


def owner_terms(picked, e_pick, live, cond_block, e_cond, table_a, table_b):
    slots = picked.shape[0]
    pair_real = (
        picked[:, None, :].astype(jnp.float32) * cond_block[None].astype(jnp.float32)
    ).astype(jnp.bfloat16)
    count = slots * cond_block.shape[0]
    rows = pair_real.reshape(count * GA, GB)
    first = jnp.dot(rows, table_b.T, preferred_element_type=jnp.float32).astype(jnp.bfloat16)
    first = first.reshape(count, GA, GB)
    moved = jnp.einsum("ja,pak->pjk", table_a, first, preferred_element_type=jnp.float32)
    moved = moved.astype(jnp.bfloat16).reshape(count, GA * GB)
    weight = live[:, None] * 2.0 / (e_cond[None, :] - e_pick[:, None])
    weighted = (moved[:, :WIN].astype(jnp.float32) * weight.reshape(count, 1)).astype(jnp.bfloat16)
    return (moved, weighted)


def shards(cond_orbitals, cond_energy, val_orbitals, val_energy, val_slots, owner_count):
    cond_block = lax.all_to_all(cond_orbitals, "pair", split_axis=2, concat_axis=1, tiled=True)[0].T
    all_orb, all_energy = (
        lax.all_gather(val_orbitals, ("ka", "pair"), axis=0, tiled=True),
        lax.all_gather(val_energy, ("ka", "pair"), axis=0, tiled=True),
    )
    slots = val_slots[0, 0]
    picked = jnp.take(all_orb, slots, axis=0)
    e_pick = jnp.take(all_energy, slots).astype(jnp.float32)
    live = (lax.iota(jnp.int32, slots.shape[0]) < owner_count[0, 0]).astype(jnp.float32)
    moved, weighted = owner_terms(
        picked, e_pick, live, cond_block, cond_energy[0], cosine_table(GA), cosine_table(GB)
    )
    owners = lax.axis_size("pair")
    mine = lax.psum_scatter(
        lax.dot_general(
            moved, weighted, (((0,), (0,)), ((), ())), preferred_element_type=jnp.float32
        ),
        "pair",
        scatter_dimension=0,
        tiled=True,
    )
    scale = 2.0 / (SLOTS * BC * owners)
    return (mine * scale)[None]


def solution(mesh):
    return jax.shard_map(
        shards,
        mesh=mesh,
        in_specs=(
            P("ka", "pair", None),
            P("ka", "pair"),
            P(("ka", "pair"), None),
            P(("ka", "pair")),
            P("ka", "pair", None),
            P("ka", "pair"),
        ),
        out_specs=P("ka", "pair", None),
        check_vma=False,
    )
```

profile of v0, /device:TPU:0, one launch (start us, length us, event | category | flops | bytes accessed | tf_op | source)
XLA Modules:
  0.0 298.1 jit_solution(10170052519686423794)
XLA Ops:
  6.5 2.3 copy.15
  8.9 0.5 broadcast.173
  9.4 11.5 %reduce = bf16[2048,128]{1,0:T(8,128)(2,1)S(1)} reduce(bf16[2048,1,128]{2,1,0:T(2,128)(2,1)S(1)} %bitcast.43, bf16[]{:T(256)} %broadcast.173), dimensions={1}, to_apply=%bitcast.30.reduce_sub_computation | reduce | bytes 1048578
  20.9 0.9 reshape.162
  21.8 8.3 %all-to-all-start = ((bf16[16,2,8192]{2,1,0:T(2,128)(2,1)}), bf16[16,2,8192]{2,1,0:T(2,128)(2,1)S(1)}, u32[]{:S(2)}, u32[]{:S(2)}) async-start(bf16[16,2,8192]{2,1,0:T(2,128)(2,1)} %reshape.162), calls=%async_computation | async-start | bytes 1048576 | tf_op jit(solution)/shard_map/all_to_all | solution.py:37
  30.2 0.0 reduce-scatter.2.cloned.1.call-start
  30.3 0.7 fusion.11
  31.6 0.1 dynamic-update-slice
  31.7 41.0 %all-reduce = bf16[32]{0:T(256)(128)(2,1)S(1)} all-reduce(bf16[32]{0:T(256)(128)(2,1)S(1)} %dynamic-update-slice), channel_id=1, replica_groups=mesh['ka'=2,'pair'=16] {'ka','pair'}, use_global_device_ids=true, to_apply=%add | all-reduce | flops 32 | bytes 128
  72.7 67.5 %all-gather = bf16[32,1,2048]{2,1,0:T(2,128)(2,1)S(1)} all-gather(bf16[1,1,2048]{2,1,0:T(2,128)(2,1)} %bitcast.47), channel_id=1, replica_groups=mesh['ka'=2,'pair'=16] {'ka','pair'}, dimensions={0}, use_global_device_ids=true | all-gather | bytes 135168 | tf_op jit(solution)/shard_map/all_gather | solution.py:39
  140.2 0.1 copy.24
  140.3 0.7 gather_fusion.1
  141.0 0.6 gather_fusion
  142.2 0.7 select_convert_fusion.1
  142.9 0.7 divide_bitcast_fusion
  143.6 0.1 select_convert_fusion
  143.7 0.0 all-to-all-done
  143.7 0.5 reshape.163
  144.3 0.1 copy.16
  144.3 0.1 convert_bitcast_fusion
  144.4 0.3 copy.17
  144.8 0.3 copy.18
  145.1 5.4 %multiply_convert_fusion = bf16[16,128,2048]{2,1,0:T(8,128)(2,1)} fusion(f32[128,2048]{1,0:T(8,128)S(1)} %copy.18, f32[16,2048]{1,0:T(8,128)S(1)} %select_convert_fusion), kind=kLoop, calls=%fused_computation.3 | loop fusion | flops 8388608 | bytes 9568256 | tf_op jit(solution)/shard_map/convert_element_type | solution.py:24
  150.5 13.5 %convert_element_type.68 = bf16[32768,128]{1,0:T(8,128)(2,1)} reshape(bf16[16,128,2048]{2,1,0:T(8,128)(2,1)} %multiply_convert_fusion) | data formatting | bytes 16777216 | tf_op jit(solution)/shard_map/convert_element_type | solution.py:24
  164.0 5.9 %convolution_convert_fusion = bf16[32768,128]{1,0:T(8,128)(2,1)S(1)} fusion(bf16[32768,128]{1,0:T(8,128)(2,1)} %convert_element_type.68, f32[128]{0:T(128)S(1)} %get-tuple-element.8, f32[128]{0:T(128)S(1)} %get-tuple-element.7), kind=kOutput, calls=%fused_computation.2 | convolution fusion | flops 1078001664 | bytes 16778240 | tf_op jit(solution)/shard_map/dot_general | solution.py:27
  169.9 5.6 %convolution_convert_fusion.1 = bf16[2048,128,16]{1,2,0:T(8,128)(2,1)} fusion(bf16[2048,16,128]{2,1,0:T(8,128)(2,1)S(1)} %bitcast.39, f32[16]{0:T(128)S(1)} %get-tuple-element.10, f32[16]{0:T(128)S(1)} %get-tuple-element.9), kind=kOutput, calls=%fused_computation.5 | convolution fusion | flops 138413056 | bytes 16777344 | tf_op jit(solution)/shard_map/ja,pak->pjk/dot_general | solution.py:29
  175.5 10.9 %copy.23 = bf16[256,8,16,128]{3,1,2,0:T(8,128)(2,1)} copy(bf16[256,8,16,128]{3,2,1,0:T(8,128)(2,1)} %bitcast.40) | data formatting | bytes 16777216
  186.4 10.6 %fusion = f32[2048,512]{1,0:T(8,128)} fusion(bf16[2048,2048]{1,0:T(8,128)(2,1)} %bitcast.41, f32[2048]{0:T(1024)S(1)} %divide_bitcast_fusion), kind=kOutput, calls=%fused_computation.7 | convolution fusion | flops 4298113024 | bytes 14688256 | tf_op jit(solution)/shard_map/dot_general | solution.py:51
  197.0 0.0 reduce-scatter.2.cloned.1.call-update
  197.0 92.6 %reduce-scatter.2.cloned.1.call-done = f32[128,512]{1,0:T(8,128)} async-done(((f32[2048,512]{1,0:T(8,128)}), f32[128,512]{1,0:T(8,128)}) %reduce-scatter.2.cloned.1.call-update) | async-done | bytes 262160 | tf_op jit(solution)/shard_map/reduce_scatter | solution.py:50
  289.6 1.7 multiply_bitcast_fusion
  (5 shorter events, 0.0 us)
Async XLA Ops:
  21.8 121.9 %all-to-all-start = ((bf16[16,2,8192]{2,1,0:T(2,128)(2,1)}), bf16[16,2,8192]{2,1,0:T(2,128)(2,1)S(1)}, u32[]{:S(2)}, u32[]{:S(2)}) async-start(bf16[16,2,8192]{2,1,0:T(2,128)(2,1)} %reshape.162), calls=%async_computation | async-start | bytes 1048576 | tf_op jit(solution)/shard_map/all_to_all | solution.py:37
  30.2 259.4 %reduce-scatter.2.cloned.1.call-start = ((), (), s32[]{:S(2)}) async-start(), calls=%async_computation.2 | async-start | bytes 4456448 | tf_op jit(solution)/shard_map/reduce_scatter | solution.py:50
Sparse Core Ops, SparseCore 0:
  197.1 92.4 reduce-scatter.1
where the time goes:
time: 299 us; the launch traced here: 298 us
  blocking collectives  108 us (36%)
  waiting for transfers between devices  92.6 us (31%)
  local copies, waits for them, and re-layouts  30.9 us (10%)
  matrix products  22.1 us (7%)
  other arithmetic  20.8 us (7%)
  between operations  14.8 us (5%)
  starting transfers between devices  8.38 us (3%)
    reduce_scatter x1, waiting for transfers between devices, shards(): lax.psum_scatter(lax.dot_general(moved, weighted, (((0,), (0,)), ((), ())...  92.6 us
    all_gather x1, blocking collectives, shards(): lax.all_gather(val_orbitals, ('ka', 'pair'), axis=0, tiled=True)  67.5 us
    unnamed x1, blocking collectives  41 us
    unnamed x8, local copies, waits for them, and re-layouts  15.4 us
    convert_element_type x1, local copies, waits for them, and re-layouts, owner_terms(): pair_real = (picked[:, None, :].astype(jnp.float32) * cond_block[None].as...  13.5 us
    unnamed x1, other arithmetic  11.5 us
    dot_general x1, matrix products, shards(): lax.dot_general(moved, weighted, (((0,), (0,)), ((), ())), preferred_elem...  10.6 us
    all_to_all x1, starting transfers between devices, shards(): lax.all_to_all(cond_orbitals, 'pair', split_axis=2, concat_axis=1, tiled=...  8.34 us
  transfers between devices with their start and end apart: 2, of which 1 were waited for; matrix products, arithmetic and copies ran while one was open for 1% of the time, Pallas kernels for 0%

commit v1 on v0

v1 whole, which is shorter than its diff:
```python
import functools

import jax
import jax.numpy as jnp
import numpy as np
from jax import lax
from jax.experimental import pallas as pl
from jax.experimental.pallas import tpu as pltpu
from jax.sharding import PartitionSpec as P

GA = 16
GB = 128
MESH = pl.DeviceIdType.MESH
F32 = jnp.float32
BF16 = jnp.bfloat16


def cosine_table(length):
    freq = lax.iota(jnp.float32, length)[:, None]
    point = lax.iota(jnp.float32, length)[None, :]
    factor = jnp.where(freq == 0, jnp.sqrt(1.0 / length), jnp.sqrt(2.0 / length))
    return (factor * jnp.cos(jnp.pi * (point + 0.5) * freq / length)).astype(jnp.bfloat16)


def kernel(
    ka_size, n, scale,
    slots_ref, count_ref, ec_ref, msg_ref, tb_ref, t2_ref, cond_ref,
    out_ref,
    vals, cblk, pk, wrow, first, moved, wt,
    part_a, part_b, got1_a, got1_b, send2_a, send2_b, got2_a, got2_b, send3, got3,
    v_send, v_recv, c_send, c_recv, s1, r1, s2, r2, s3, r3,
):
    my_ka = lax.axis_index("ka")
    me = lax.axis_index("pair")
    flat = my_ka * n + me
    devices = ka_size * n
    slots = slots_ref.shape[0]
    bc = ec_ref.shape[1]
    rows = cond_ref.shape[0]
    win = out_ref.shape[1]
    half = win // 2
    groups = n // 4
    per_a = n // GA
    rb = GB // 8

    barrier = pltpu.get_barrier_semaphore()

    def greet(i, carry):
        other = lax.rem(flat + i, devices)
        pl.semaphore_signal(
            barrier, inc=1, device_id=(other // n, lax.rem(other, n)), device_id_type=MESH
        )
        return carry

    lax.fori_loop(1, devices, greet, 0)
    own_val = pltpu.make_async_copy(msg_ref, vals.at[flat], c_send.at[me])
    own_val.start()
    own_cond = pltpu.make_async_copy(
        cond_ref.at[:, pl.ds(pl.multiple_of(me * bc, bc), bc)], cblk.at[me], c_recv.at[me]
    )
    own_cond.start()
    pl.semaphore_wait(barrier, devices - 1)

    def send_val(i, carry):
        other = lax.rem(flat + i, devices)
        pltpu.make_async_remote_copy(
            src_ref=msg_ref, dst_ref=vals.at[flat], send_sem=v_send, recv_sem=v_recv,
            device_id=(other // n, lax.rem(other, n)), device_id_type=MESH,
        ).start()
        return carry

    lax.fori_loop(1, devices, send_val, 0)

    def cond_copy(dest, slot):
        return pltpu.make_async_remote_copy(
            src_ref=cond_ref.at[:, pl.ds(pl.multiple_of(dest * bc, bc), bc)],
            dst_ref=cblk.at[slot], send_sem=c_send.at[dest], recv_sem=c_recv.at[slot],
            device_id=(my_ka, dest), device_id_type=MESH,
        )

    def send_cond(i, carry):
        cond_copy(lax.rem(me + i, n), me).start()
        return carry

    lax.fori_loop(1, n, send_cond, 0)

    own_val.wait()
    rest = vals.at[pl.ds(0, devices - 1)]
    pltpu.make_async_copy(rest, rest, v_recv).wait()

    count = count_ref[0]
    for s in range(slots):
        tile = vals[slots_ref[s]]
        pk[:, s, :] = tile[:GA].astype(F32)
        e_v = tile[GA : GA + 1].astype(F32)
        live = jnp.where(jnp.full((1, bc), s, jnp.int32) < count, 1.0, 0.0)
        wrow[0:1, s * bc : (s + 1) * bc] = live * 2.0 / (ec_ref[...] - e_v)

    my_a = me // per_a

    def do_first(i, carry):
        a = lax.rem(my_a + GA - i, GA)
        for r in range(per_a):
            src = a * per_a + r
            pltpu.make_async_copy(cblk.at[src], cblk.at[src], c_recv.at[src]).wait()
        block = cblk[pl.ds(a * per_a, per_a)].reshape(GB, bc).astype(F32)
        cols = pk[a].T
        for pair in range(slots // 2):
            x = jnp.concatenate(
                [(block * cols[:, s : s + 1]).astype(BF16) for s in (2 * pair, 2 * pair + 1)],
                axis=1,
            )
            f = jnp.dot(tb_ref[...], x, preferred_element_type=F32).astype(BF16)
            for kg in range(8):
                first[
                    kg, pl.ds(pl.multiple_of(a * rb, rb), rb), pair * 2 * bc : (pair + 1) * 2 * bc
                ] = f[kg * rb : (kg + 1) * rb]
        return carry

    lax.fori_loop(0, GA, do_first, 0)

    def do_moved(kg, carry):
        at = pl.multiple_of(kg * rb, rb)
        for pc in range(slots // 2):
            sl = slice(pc * 2 * bc, (pc + 1) * 2 * bc)
            mv = jnp.dot(t2_ref[...], first[kg, :, sl], preferred_element_type=F32).astype(BF16)
            for j in range(GA):
                piece = mv[j * rb : (j + 1) * rb]
                moved[pl.ds(j * GB + at, rb), sl] = piece
                if j * GB < win:
                    wt[pl.ds(j * GB + at, rb), sl] = (
                        piece.astype(F32) * wrow[0:1, sl]
                    ).astype(BF16)
        return carry

    lax.fori_loop(0, 8, do_moved, 0)

    mz = me // 4
    my = lax.rem(me, 4) // 2
    mx = lax.rem(me, 2)
    px, py = 1 - mx, 1 - my
    x_peer = mz * 4 + my * 2 + px
    y_peer = mz * 4 + py * 2 + mx

    def remote(src, dst, ssem, rsem, dest):
        return pltpu.make_async_remote_copy(
            src_ref=src, dst_ref=dst, send_sem=ssem, recv_sem=rsem,
            device_id=(my_ka, dest), device_id_type=MESH,
        )

    def step1(t):
        return (
            remote(part_a.at[px, t], got1_a.at[t], s1.at[0, t], r1.at[0, t], x_peer),
            remote(part_b.at[py, t], got1_b.at[t], s1.at[1, t], r1.at[1, t], y_peer),
        )

    def step2(t):
        return (
            remote(send2_a.at[t], got2_a.at[t], s2.at[0, t], r2.at[0, t], y_peer),
            remote(send2_b.at[t], got2_b.at[t], s2.at[1, t], r2.at[1, t], x_peer),
        )

    def step3(t):
        dest = lax.rem(mz + 1 + t, groups) * 4 + my * 2 + mx
        return remote(send3.at[t], got3.at[t], s3.at[t], r3.at[t], dest)

    def both(t):
        a = part_a[mx, t, my].astype(F32) + got1_a[t, my].astype(F32) + got2_a[t].astype(F32)
        b = part_b[my, t, mx].astype(F32) + got1_b[t, mx].astype(F32) + got2_b[t].astype(F32)
        return a, b

    def flow(i, carry):
        @pl.when(i < groups)
        def _():
            t = i
            z = lax.rem(mz + 1 + t, groups)
            lhs = moved[pl.ds(pl.multiple_of(z * 4 * rows, 4 * rows), 4 * rows), :]
            for h in range(2):
                acc = lax.dot_general(
                    lhs, wt[h * half : (h + 1) * half, :], (((1,), (1,)), ((), ())),
                    preferred_element_type=F32,
                ).astype(BF16)
                for y in range(2):
                    for x in range(2):
                        piece = acc[(2 * y + x) * rows : (2 * y + x + 1) * rows]
                        if h == 0:
                            part_a[x, t, y] = piece
                        else:
                            part_b[y, t, x] = piece
                step1(t)[h].start()

        @pl.when((i >= 2) & (i < groups + 2))
        def _():
            t = i - 2
            first_a, first_b = step1(t)
            second_a, second_b = step2(t)
            first_a.wait_recv()
            send2_a[t] = (part_a[mx, t, py].astype(F32) + got1_a[t, py].astype(F32)).astype(BF16)
            second_a.start()
            first_b.wait_recv()
            send2_b[t] = (part_b[my, t, px].astype(F32) + got1_b[t, px].astype(F32)).astype(BF16)
            second_b.start()

        @pl.when((i >= 4) & (i < groups + 3))
        def _():
            t = i - 4
            for copy in step2(t):
                copy.wait_recv()
            a, b = both(t)
            send3[t, :, :half] = a.astype(BF16)
            send3[t, :, half:] = b.astype(BF16)
            step3(t).start()

        return carry

    lax.fori_loop(0, groups + 3, flow, 0)

    last = groups - 1
    for copy in step2(last):
        copy.wait_recv()
    a, b = both(last)
    for t in range(groups - 1):
        step3(t).wait_recv()
        a = a + got3[t, :, :half].astype(F32)
        b = b + got3[t, :, half:].astype(F32)
    out_ref[:, :half] = a * scale
    out_ref[:, half:] = b * scale

    pltpu.make_async_copy(rest, rest, v_send).wait()

    def drain_cond(i, carry):
        cond_copy(lax.rem(me + i, n), me).wait_send()
        return carry

    lax.fori_loop(1, n, drain_cond, 0)

    def drain(t, carry):
        for copy in step1(t) + step2(t):
            copy.wait_send()
        return carry

    lax.fori_loop(0, groups, drain, 0)
    for t in range(groups - 1):
        step3(t).wait_send()


def shards(ka_size, n, cond_orbitals, cond_energy, val_orbitals, val_energy, val_slots, owner_count):
    cond = cond_orbitals[0]
    rows, bc = cond.shape[0], cond.shape[1] // n
    slots = val_slots.shape[2]
    win = 4 * GB
    half = win // 2
    grid = GA * GB
    count = slots * bc
    groups = n // 4
    msg = jnp.concatenate(
        [val_orbitals.reshape(GA, GB), jnp.broadcast_to(val_energy[:, None], (GA, GB))], axis=0
    )
    table_b = cosine_table(GB)
    rb = GB // 8
    table_2 = (
        cosine_table(GA)[:, None, :, None] * jnp.eye(rb, dtype=BF16)[None, :, None, :]
    ).reshape(GA * rb, GA * rb)
    scale = 2.0 / (slots * bc * n)
    vmem = pl.BlockSpec(memory_space=pltpu.VMEM)
    smem = pl.BlockSpec(memory_space=pltpu.SMEM)
    dma = pltpu.SemaphoreType.DMA
    out = pl.pallas_call(
        functools.partial(kernel, ka_size, n, scale),
        out_shape=jax.ShapeDtypeStruct((rows, win), F32),
        in_specs=[smem, smem, vmem, vmem, vmem, vmem, pl.BlockSpec(memory_space=pl.ANY)],
        out_specs=vmem,
        scratch_shapes=[
            pltpu.VMEM((ka_size * n, 2 * GA, GB), BF16),
            pltpu.VMEM((n, rows, bc), BF16),
            pltpu.VMEM((GA, slots, GB), F32),
            pltpu.VMEM((8, count), F32),
            pltpu.VMEM((8, GA * rb, count), BF16),
            pltpu.VMEM((grid, count), BF16),
            pltpu.VMEM((win, count), BF16),
            pltpu.VMEM((2, groups, 2, rows, half), BF16),
            pltpu.VMEM((2, groups, 2, rows, half), BF16),
            pltpu.VMEM((groups, 2, rows, half), BF16),
            pltpu.VMEM((groups, 2, rows, half), BF16),
            pltpu.VMEM((groups, rows, half), BF16),
            pltpu.VMEM((groups, rows, half), BF16),
            pltpu.VMEM((groups, rows, half), BF16),
            pltpu.VMEM((groups, rows, half), BF16),
            pltpu.VMEM((groups, rows, win), BF16),
            pltpu.VMEM((groups, rows, win), BF16),
            dma(()), dma(()), dma((n,)), dma((n,)),
            dma((2, groups)), dma((2, groups)), dma((2, groups)), dma((2, groups)),
            dma((groups,)), dma((groups,)),
        ],
        compiler_params=pltpu.CompilerParams(
            collective_id=0, has_side_effects=True, vmem_limit_bytes=60 * 1024 * 1024
        ),
        name="polarizability",
    )(val_slots[0, 0], owner_count[0], cond_energy, msg, table_b, table_2, cond)
    return out[None]


def solution(mesh):
    return jax.shard_map(
        functools.partial(shards, mesh.shape["ka"], mesh.shape["pair"]),
        mesh=mesh,
        in_specs=(
            P("ka", "pair", None),
            P("ka", "pair"),
            P(("ka", "pair"), None),
            P(("ka", "pair")),
            P("ka", "pair", None),
            P("ka", "pair"),
        ),
        out_specs=P("ka", "pair", None),
        check_vma=False,
    )
```

time: 299 us -> 69.3 us (0.23)
  blocking collectives: 108 us -> 0 us
  waiting for transfers between devices: 92.6 us -> 0 us
  Pallas kernels: 0 us -> 62.3 us
  local copies, waits for them, and re-layouts: 30.9 us -> 3.92 us
  matrix products: 22.1 us -> 0 us
  other arithmetic: 20.8 us -> 1.13 us
  between operations: 14.8 us -> 1.33 us
  starting transfers between devices: 8.38 us -> 0 us
    reduce_scatter x1 -> x0, waiting for transfers between devices: 92.6 us -> none  [shards(): lax.psum_scatter(lax.dot_general(moved, weighted, (((0,), (0,)), ((), ())...]
    all_gather x1 -> x0, blocking collectives: 67.5 us -> none  [shards(): lax.all_gather(val_orbitals, ('ka', 'pair'), axis=0, tiled=True)]
    pallas_call x0 -> x1, Pallas kernels: none -> 62.3 us  [shards(): pl.pallas_call(functools.partial(kernel, ka_size, n, scale), out_shape=ja...]
    unnamed x1 -> x0, blocking collectives: 41 us -> none
    dot_general x3 -> x0, matrix products: 22.1 us -> none  [the longest x1 10.6 us: shards(): lax.dot_general(moved, weighted, (((0,), (0,)), ((), ())), preferred_elem...]
    convert_element_type x3 -> x0, local copies, waits for them, and re-layouts: 14.1 us -> none  [the longest x1 13.5 us: owner_terms(): pair_real = (picked[:, None, :].astype(jnp.float32) * cond_block[None].as...]
    unnamed x8 -> x3, local copies, waits for them, and re-layouts: 15.4 us -> 1.68 us
    unnamed x1, other arithmetic: 11.5 us -> 0.03 us
  transfers between devices with their start and end apart: 2 -> 0, of which waited for: 1 -> 0; matrix products, arithmetic and copies ran while one was open for 1% -> 0% of each run, Pallas kernels for 0% -> 0%
where the time goes in v1:
time: 69.3 us; the launch traced here: 68.6 us
  Pallas kernels  62.3 us (90%)
  local copies, waits for them, and re-layouts  3.92 us (6%)
  between operations  1.33 us (2%)
  other arithmetic  1.13 us (2%)
    pallas_call x1, Pallas kernels, shards(): pl.pallas_call(functools.partial(kernel, ka_size, n, scale), out_shape=ja...  62.3 us
    unnamed x3, local copies, waits for them, and re-layouts  1.68 us
    mul x1, local copies, waits for them, and re-layouts, shards(): cosine_table(GA)[:, None, :, None]  1.65 us

profile of v1, /device:TPU:0, one launch (start us, length us, event | category | flops | bytes accessed | tf_op | source)
XLA Modules:
  0.0 68.6 jit_solution(2033702335984579259)
XLA Ops:
  0.0 0.1 multiply_convert_fusion.1
  0.1 0.1 broadcast_multiply_fusion
  0.2 1.7 %mul.102.t2_ref = bf16[256,256]{1,0:T(8,128)(2,1)} reshape(bf16[16,16,16,16]{3,2,1,0:T(8,128)(2,1)S(1)} %broadcast_multiply_fusion) | data formatting | bytes 262144 | tf_op jit(solution)/shard_map/mul | solution.py:262
  1.9 0.0 copy-start
  1.9 0.9 %multiply_convert_fusion.tb_ref = bf16[128,128]{1,0:T(8,128)(2,1)} fusion(f32[128]{0:T(128)S(1)} %get-tuple-element.6, f32[128]{0:T(128)S(1)} %get-tuple-element.5), kind=kLoop, calls=%fused_computation.1 | loop fusion | flops 65536 | bytes 33792 | tf_op jit(solution)/shard_map/convert_element_type | solution.py:22
  2.8 0.0 copy-done
  3.5 0.6 concatenate.3.msg_ref
  4.7 62.3 %polarizability.1 = f32[128,512]{1,0:T(8,128)} custom-call(s32[16]{0:T(128)} %bitcast.13, s32[1]{0:T(128)} %bitcast.9.count_ref, f32[1,128]{1,0:T(1,128)} %ec_ref.1, bf16[32,128]{1,0:T(8,128)(2,1)} %concatenate.3.msg_ref, bf16[128,128]{1,0:T(8,128)(2,1)} %multiply_convert_fusion.tb_ref, bf16[256,256]{1,0:T(8,128)(2,1)} %mul.102.t2_ref, ...), custom_call_target="tpu_custom_call" | custom-call | tf_op jit(solution)/shard_map/polarizability/pallas_call | solution.py:268
  67.0 1.7 %copy.10 = f32[1,128,512]{2,1,0:T(8,128)} copy(f32[1,128,512]{2,1,0:T(8,128)} %bitcast.10) | data formatting | bytes 524288
  (4 shorter events, 0.1 us)
Async XLA Ops:
  1.9 0.9 %copy-start = (bf16[1,2048]{1,0:T(2,128)(2,1)S(1)}, bf16[1,2048]{1,0:T(2,128)(2,1)}, u32[]{:S(2)}) copy-start(bf16[1,2048]{1,0:T(2,128)(2,1)} %param.8) | copy-start | bytes 12292

commit v2 on v1

v2 whole, which is shorter than its diff:
```python
import functools

import jax
import jax.numpy as jnp
import numpy as np
from jax import lax
from jax.experimental import pallas as pl
from jax.experimental.pallas import tpu as pltpu
from jax.sharding import PartitionSpec as P

GA = 16
GB = 128
LAGS = (2, 4)
MESH = pl.DeviceIdType.MESH
F32 = jnp.float32
BF16 = jnp.bfloat16


def cosine_table(length):
    freq = np.arange(length, dtype=np.float32)[:, None]
    point = np.arange(length, dtype=np.float32)[None, :]
    factor = np.where(freq == 0, np.sqrt(np.float32(1.0 / length)), np.sqrt(np.float32(2.0 / length)))
    angle = np.float32(np.pi) * (point + np.float32(0.5)) * freq / np.float32(length)
    return (factor * np.cos(angle)).astype(jnp.bfloat16)


def xor(value, other):
    out = 0
    for bit in (1, 2, 4, 8, 16, 32, 64, 128):
        out = out + lax.rem(value // bit + other // bit, 2) * bit
    return out


def kernel(
    ka_size, n, scale,
    slots_ref, count_ref, ec_ref, msg_ref, tb_ref, t2_ref, cond_ref,
    out_ref,
    vals, cblk, pk, wrow, first, moved, wt,
    part_a, part_b, got1_a, got1_b, send2_a, send2_b, got2_a, got2_b, send3, got3,
    v_own, v_send, v_recv, l_send, l_recv, c_send, c_recv, s1, r1, s2, r2, s3, r3,
):
    my_ka = lax.axis_index("ka")
    me = lax.axis_index("pair")
    slots = slots_ref.shape[0]
    bc = ec_ref.shape[1]
    rows = cond_ref.shape[0]
    win = out_ref.shape[1]
    half = win // 2
    groups = n // 4
    per_a = n // GA
    rb = GB // 8

    barrier = pltpu.get_barrier_semaphore()

    def greet(c, carry):
        pl.semaphore_signal(barrier, inc=1, device_id=(my_ka, xor(me, c)), device_id_type=MESH)
        return carry

    def greet_core(c, carry):
        pl.semaphore_signal(
            barrier, inc=1, device_id=(lax.rem(my_ka + c, ka_size), me), device_id_type=MESH
        )
        return carry

    lax.fori_loop(1, n, greet, 0)
    lax.fori_loop(1, ka_size, greet_core, 0)
    own_val = pltpu.make_async_copy(msg_ref, vals.at[my_ka, me], v_own)
    own_val.start()
    own_cond = pltpu.make_async_copy(
        cond_ref.at[:, pl.ds(pl.multiple_of(me * bc, bc), bc)], cblk.at[me], c_recv.at[me]
    )
    own_cond.start()
    pl.semaphore_wait(barrier, n + ka_size - 2)

    def send_val(c, carry):
        pltpu.make_async_remote_copy(
            src_ref=msg_ref, dst_ref=vals.at[my_ka, me], send_sem=v_send, recv_sem=v_recv,
            device_id=(my_ka, xor(me, c)), device_id_type=MESH,
        ).start()
        return carry

    lax.fori_loop(1, n, send_val, 0)

    def cond_copy(dest, slot):
        return pltpu.make_async_remote_copy(
            src_ref=cond_ref.at[:, pl.ds(pl.multiple_of(dest * bc, bc), bc)],
            dst_ref=cblk.at[slot], send_sem=c_send.at[dest], recv_sem=c_recv.at[slot],
            device_id=(my_ka, dest), device_id_type=MESH,
        )

    def send_cond(c, carry):
        cond_copy(xor(me, c), me).start()
        return carry

    lax.fori_loop(1, 4, send_cond, 0)
    lax.fori_loop(n // 2, n, send_cond, 0)
    lax.fori_loop(4, n // 2, send_cond, 0)

    own_val.wait()
    rest = vals.at[my_ka, pl.ds(0, n - 1)]
    pltpu.make_async_copy(rest, rest, v_recv).wait()

    def lane_copy(c):
        other = lax.rem(my_ka + c, ka_size)
        return pltpu.make_async_remote_copy(
            src_ref=vals.at[my_ka], dst_ref=vals.at[my_ka],
            send_sem=l_send.at[other], recv_sem=l_recv.at[my_ka],
            device_id=(other, me), device_id_type=MESH,
        )

    def send_lane(c, carry):
        lane_copy(c).start()
        return carry

    def wait_lane(c, carry):
        other = lax.rem(my_ka + c, ka_size)
        pltpu.make_async_copy(vals.at[other], vals.at[other], l_recv.at[other]).wait()
        return carry

    lax.fori_loop(1, ka_size, send_lane, 0)
    lax.fori_loop(1, ka_size, wait_lane, 0)

    count = count_ref[0]
    for s in range(slots):
        tile = vals[slots_ref[s] // n, lax.rem(slots_ref[s], n)]
        pk[:, s, :] = tile[:GA].astype(F32)
        e_v = tile[GA : GA + 1].astype(F32)
        live = jnp.where(jnp.full((1, bc), s, jnp.int32) < count, 1.0, 0.0)
        wrow[0:1, s * bc : (s + 1) * bc] = live * 2.0 / (ec_ref[...] - e_v)

    my_a = me // per_a

    def do_first(i, carry):
        a = xor(my_a, i)
        for r in range(per_a):
            src = a * per_a + r
            pltpu.make_async_copy(cblk.at[src], cblk.at[src], c_recv.at[src]).wait()
        block = cblk[pl.ds(a * per_a, per_a)].reshape(GB, bc).astype(F32)
        cols = pk[a].T
        for pair in range(slots // 2):
            x = jnp.concatenate(
                [(block * cols[:, s : s + 1]).astype(BF16) for s in (2 * pair, 2 * pair + 1)],
                axis=1,
            )
            f = jnp.dot(tb_ref[...], x, preferred_element_type=F32).astype(BF16)
            for kg in range(8):
                first[
                    kg, pl.ds(pl.multiple_of(a * rb, rb), rb), pair * 2 * bc : (pair + 1) * 2 * bc
                ] = f[kg * rb : (kg + 1) * rb]
        return carry

    lax.fori_loop(0, GA // 4, do_first, 0)
    lax.fori_loop(GA // 2, 3 * GA // 4, do_first, 0)
    lax.fori_loop(GA // 4, GA // 2, do_first, 0)
    lax.fori_loop(3 * GA // 4, GA, do_first, 0)

    def do_moved(kg, carry):
        at = pl.multiple_of(kg * rb, rb)
        for pc in range(slots // 2):
            sl = slice(pc * 2 * bc, (pc + 1) * 2 * bc)
            mv = jnp.dot(t2_ref[...], first[kg, :, sl], preferred_element_type=F32).astype(BF16)
            for j in range(GA):
                piece = mv[j * rb : (j + 1) * rb]
                moved[pl.ds(j * GB + at, rb), sl] = piece
                if j * GB < win:
                    wt[pl.ds(j * GB + at, rb), sl] = (
                        piece.astype(F32) * wrow[0:1, sl]
                    ).astype(BF16)
        return carry

    lax.fori_loop(0, 8, do_moved, 0)

    mz = me // 4
    my = lax.rem(me, 4) // 2
    mx = lax.rem(me, 2)
    px, py = 1 - mx, 1 - my
    x_peer = mz * 4 + my * 2 + px
    y_peer = mz * 4 + py * 2 + mx

    def remote(src, dst, ssem, rsem, dest):
        return pltpu.make_async_remote_copy(
            src_ref=src, dst_ref=dst, send_sem=ssem, recv_sem=rsem,
            device_id=(my_ka, dest), device_id_type=MESH,
        )

    def step1(t):
        return (
            remote(part_a.at[px, t], got1_a.at[t], s1.at[0, t], r1.at[0, t], x_peer),
            remote(part_b.at[py, t], got1_b.at[t], s1.at[1, t], r1.at[1, t], y_peer),
        )

    def step2(t):
        return (
            remote(send2_a.at[t], got2_a.at[t], s2.at[0, t], r2.at[0, t], y_peer),
            remote(send2_b.at[t], got2_b.at[t], s2.at[1, t], r2.at[1, t], x_peer),
        )

    def step3(t):
        dest = lax.rem(mz + 1 + t // 2, groups) * 4 + my * 2 + mx
        return remote(send3.at[t], got3.at[t], s3.at[t], r3.at[t], dest)

    def both(t):
        a = part_a[mx, t, my].astype(F32) + got1_a[t, my].astype(F32) + got2_a[t].astype(F32)
        b = part_b[my, t, mx].astype(F32) + got1_b[t, mx].astype(F32) + got2_b[t].astype(F32)
        return a, b

    chunks = 2 * groups
    far = chunks - 2
    lag2, lag3 = LAGS

    def flow(i, carry):
        @pl.when(i < chunks)
        def _():
            t = i
            z = lax.rem(mz + 1 + t // 2, groups)
            col = pl.multiple_of(lax.rem(t, 2) * half, half)
            acc = lax.dot_general(
                moved[pl.ds(pl.multiple_of(z * 4 * rows, 4 * rows), 4 * rows), :],
                wt[pl.ds(col, half), :], (((1,), (1,)), ((), ())),
                preferred_element_type=F32,
            ).astype(BF16)
            for y in range(2):
                for x in range(2):
                    piece = acc[(2 * y + x) * rows : (2 * y + x + 1) * rows]
                    part_a[x, t, y] = piece[:, : half // 2]
                    part_b[y, t, x] = piece[:, half // 2 :]
            for copy in step1(t):
                copy.start()

        @pl.when((i >= lag2) & (i < chunks + lag2))
        def _():
            t = i - lag2
            first_a, first_b = step1(t)
            second_a, second_b = step2(t)
            first_a.wait_recv()
            send2_a[t] = (part_a[mx, t, py].astype(F32) + got1_a[t, py].astype(F32)).astype(BF16)
            second_a.start()
            first_b.wait_recv()
            send2_b[t] = (part_b[my, t, px].astype(F32) + got1_b[t, px].astype(F32)).astype(BF16)
            second_b.start()

        @pl.when((i >= lag3) & (i < far + lag3))
        def _():
            t = i - lag3
            for copy in step2(t):
                copy.wait_recv()
            a, b = both(t)
            send3[t, :, : half // 2] = a.astype(BF16)
            send3[t, :, half // 2 :] = b.astype(BF16)
            step3(t).start()

        return carry

    lax.fori_loop(0, max(chunks + lag2, far + lag3), flow, 0)

    for h in range(2):
        for copy in step2(far + h):
            copy.wait_recv()
        a, b = both(far + h)
        for t in range(h, far, 2):
            step3(t).wait_recv()
            a = a + got3[t, :, : half // 2].astype(F32)
            b = b + got3[t, :, half // 2 :].astype(F32)
        out_ref[:, h * half : h * half + half // 2] = a * scale
        out_ref[:, h * half + half // 2 : (h + 1) * half] = b * scale

    pltpu.make_async_copy(rest, rest, v_send).wait()

    def drain_cond(c, carry):
        cond_copy(xor(me, c), me).wait_send()
        return carry

    lax.fori_loop(1, n, drain_cond, 0)

    def drain(t, carry):
        for copy in step1(t) + step2(t):
            copy.wait_send()
        return carry

    def drain_lane(c, carry):
        lane_copy(c).wait_send()
        return carry

    lax.fori_loop(1, ka_size, drain_lane, 0)
    lax.fori_loop(0, chunks, drain, 0)
    for t in range(far):
        step3(t).wait_send()


def shards(ka_size, n, cond_orbitals, cond_energy, val_orbitals, val_energy, val_slots, owner_count):
    cond = cond_orbitals[0]
    rows, bc = cond.shape[0], cond.shape[1] // n
    slots = val_slots.shape[2]
    win = 4 * GB
    half = win // 2
    grid = GA * GB
    count = slots * bc
    chunks = n // 2
    msg = jnp.concatenate(
        [val_orbitals.reshape(GA, GB), jnp.broadcast_to(val_energy[:, None], (8, GB))], axis=0
    )
    table_b = cosine_table(GB)
    rb = GB // 8
    table_2 = np.kron(cosine_table(GA), np.eye(rb, dtype=np.float32)).astype(jnp.bfloat16)
    scale = 2.0 / (slots * bc * n)
    vmem = pl.BlockSpec(memory_space=pltpu.VMEM)
    smem = pl.BlockSpec(memory_space=pltpu.SMEM)
    dma = pltpu.SemaphoreType.DMA
    out = pl.pallas_call(
        functools.partial(kernel, ka_size, n, scale),
        out_shape=jax.ShapeDtypeStruct((rows, win), F32),
        in_specs=[smem, smem, vmem, vmem, vmem, vmem, pl.BlockSpec(memory_space=pl.ANY)],
        out_specs=vmem,
        scratch_shapes=[
            pltpu.VMEM((ka_size, n, GA + 8, GB), BF16),
            pltpu.VMEM((n, rows, bc), BF16),
            pltpu.VMEM((GA, slots, GB), F32),
            pltpu.VMEM((8, count), F32),
            pltpu.VMEM((8, GA * rb, count), BF16),
            pltpu.VMEM((grid, count), BF16),
            pltpu.VMEM((win, count), BF16),
            pltpu.VMEM((2, chunks, 2, rows, half // 2), BF16),
            pltpu.VMEM((2, chunks, 2, rows, half // 2), BF16),
            pltpu.VMEM((chunks, 2, rows, half // 2), BF16),
            pltpu.VMEM((chunks, 2, rows, half // 2), BF16),
            pltpu.VMEM((chunks, rows, half // 2), BF16),
            pltpu.VMEM((chunks, rows, half // 2), BF16),
            pltpu.VMEM((chunks, rows, half // 2), BF16),
            pltpu.VMEM((chunks, rows, half // 2), BF16),
            pltpu.VMEM((chunks, rows, half), BF16),
            pltpu.VMEM((chunks, rows, half), BF16),
            dma(()), dma(()), dma(()), dma((ka_size,)), dma((ka_size,)), dma((n,)), dma((n,)),
            dma((2, chunks)), dma((2, chunks)), dma((2, chunks)), dma((2, chunks)),
            dma((chunks,)), dma((chunks,)),
        ],
        compiler_params=pltpu.CompilerParams(
            collective_id=0, has_side_effects=True, vmem_limit_bytes=60 * 1024 * 1024
        ),
        name="polarizability",
    )(val_slots[0, 0], owner_count[0], cond_energy, msg, jnp.asarray(table_b), jnp.asarray(table_2), cond)
    return out[None]


def solution(mesh):
    return jax.shard_map(
        functools.partial(shards, mesh.shape["ka"], mesh.shape["pair"]),
        mesh=mesh,
        in_specs=(
            P("ka", "pair", None),
            P("ka", "pair"),
            P(("ka", "pair"), None),
            P(("ka", "pair")),
            P("ka", "pair", None),
            P("ka", "pair"),
        ),
        out_specs=P("ka", "pair", None),
        check_vma=False,
    )
```

time: 69.3 us -> 62.5 us (0.902)
  Pallas kernels: 62.3 us -> 58.6 us
  local copies, waits for them, and re-layouts: 3.92 us -> 2.27 us
  other arithmetic: 1.13 us -> 0.03 us
    pallas_call x1, Pallas kernels: 62.3 us -> 58.6 us  [shards(): pl.pallas_call(functools.partial(kernel, ka_size, n, scale), out_shape=ja...]
    mul x1 -> x0, local copies, waits for them, and re-layouts: 1.65 us -> none  [shards(): cosine_table(GA)[:, None, :, None]]
    convert_element_type x3 -> x0, other arithmetic: 0.94 us -> none  [the longest x2 0.93 us: cosine_table(): (factor * jnp.cos(jnp.pi * (point + 0.5) * freq / length)).astype(jnp.bfl...]
where the time goes in v2:
time: 62.5 us; the launch traced here: 62.3 us
  Pallas kernels  58.6 us (94%)
  local copies, waits for them, and re-layouts  2.27 us (4%)
  between operations  1.34 us (2%)
    pallas_call x1, Pallas kernels, shards(): pl.pallas_call(functools.partial(kernel, ka_size, n, scale), out_shape=ja...  58.6 us
    unnamed x3, local copies, waits for them, and re-layouts  1.68 us

profile of v2, /device:TPU:0, one launch (start us, length us, event | category | flops | bytes accessed | tf_op | source)
XLA Modules:
  0.0 62.3 jit_solution(8373454084807927360)
XLA Ops:
  0.0 0.0 copy-start
  1.3 0.0 copy-done
  1.4 0.6 concatenate.3.msg_ref
  2.0 58.6 %polarizability.1 = f32[128,512]{1,0:T(8,128)} custom-call(s32[16]{0:T(128)} %bitcast.11, s32[1]{0:T(128)} %bitcast.7.count_ref, f32[1,128]{1,0:T(1,128)} %ec_ref.1, bf16[24,128]{1,0:T(8,128)(2,1)} %concatenate.3.msg_ref, bf16[128,128]{1,0:T(8,128)(2,1)} %constant.4.clone.tb_ref, bf16[256,256]{1,0:T(8,128)(2,1)} %constant.5.clone.t2_ref, ...), custom_call_target="tpu_custom_call" | custom-call | tf_op jit(solution)/shard_map/polarizability/pallas_call | solution.py:309
  60.6 1.7 %copy.12 = f32[1,128,512]{2,1,0:T(8,128)} copy(f32[1,128,512]{2,1,0:T(8,128)} %bitcast.8) | data formatting | bytes 524288
  (1 shorter events, 0.0 us)
Async XLA Ops:
  0.0 1.3 %copy-start = (bf16[1,2048]{1,0:T(2,128)(2,1)S(1)}, bf16[1,2048]{1,0:T(2,128)(2,1)}, u32[]{:S(2)}) copy-start(bf16[1,2048]{1,0:T(2,128)(2,1)} %param.10) | copy-start | bytes 12292

commit v3 on v2

--- a/solution.py
+++ b/solution.py
@@ -92,9 +92,7 @@
         cond_copy(xor(me, c), me).start()
         return carry
 
-    lax.fori_loop(1, 4, send_cond, 0)
-    lax.fori_loop(n // 2, n, send_cond, 0)
-    lax.fori_loop(4, n // 2, send_cond, 0)
+    lax.fori_loop(1, n, send_cond, 0)
 
     own_val.wait()
     rest = vals.at[my_ka, pl.ds(0, n - 1)]
@@ -135,11 +133,11 @@
         for r in range(per_a):
             src = a * per_a + r
             pltpu.make_async_copy(cblk.at[src], cblk.at[src], c_recv.at[src]).wait()
-        block = cblk[pl.ds(a * per_a, per_a)].reshape(GB, bc).astype(F32)
+        block = cblk[pl.ds(a * per_a, per_a)].reshape(GB, bc)
         cols = pk[a].T
         for pair in range(slots // 2):
             x = jnp.concatenate(
-                [(block * cols[:, s : s + 1]).astype(BF16) for s in (2 * pair, 2 * pair + 1)],
+                [block * jnp.broadcast_to(cols[:, s : s + 1], (GB, bc)).astype(BF16) for s in (2 * pair, 2 * pair + 1)],
                 axis=1,
             )
             f = jnp.dot(tb_ref[...], x, preferred_element_type=F32).astype(BF16)
@@ -149,10 +147,7 @@
                 ] = f[kg * rb : (kg + 1) * rb]
         return carry
 
-    lax.fori_loop(0, GA // 4, do_first, 0)
-    lax.fori_loop(GA // 2, 3 * GA // 4, do_first, 0)
-    lax.fori_loop(GA // 4, GA // 2, do_first, 0)
-    lax.fori_loop(3 * GA // 4, GA, do_first, 0)
+    lax.fori_loop(0, GA, do_first, 0)
 
     def do_moved(kg, carry):
         at = pl.multiple_of(kg * rb, rb)

time: 62.5 us -> 56.2 us (0.90)
  Pallas kernels: 58.6 us -> 52.3 us
    pallas_call x1, Pallas kernels: 58.6 us -> 52.3 us  [shards(): pl.pallas_call(functools.partial(kernel, ka_size, n, scale), out_shape=ja...]
where the time goes in v3:
time: 56.2 us; the launch traced here: 56 us
  Pallas kernels  52.3 us (93%)
  local copies, waits for them, and re-layouts  2.27 us (4%)
  between operations  1.34 us (2%)
    pallas_call x1, Pallas kernels, shards(): pl.pallas_call(functools.partial(kernel, ka_size, n, scale), out_shape=ja...  52.3 us
    unnamed x3, local copies, waits for them, and re-layouts  1.68 us

profile of v3, /device:TPU:0, one launch (start us, length us, event | category | flops | bytes accessed | tf_op | source)
XLA Modules:
  0.0 56.0 jit_solution(4559530403708702440)
XLA Ops:
  0.0 0.0 copy-start
  1.3 0.0 copy-done
  1.4 0.6 %concatenate.3.msg_ref = bf16[24,128]{1,0:T(8,128)(2,1)} pad(bf16[16,128]{1,0:T(8,128)(2,1)S(1)} %bitcast.10, bf16[]{:T(256)} %bitcast.6), padding=0_8x0_0 | pad | bytes 10242 | tf_op jit(solution)/shard_map/concatenate | solution.py:294
  2.0 52.3 %polarizability.1 = f32[128,512]{1,0:T(8,128)} custom-call(s32[16]{0:T(128)} %bitcast.11, s32[1]{0:T(128)} %bitcast.7.count_ref, f32[1,128]{1,0:T(1,128)} %ec_ref.1, bf16[24,128]{1,0:T(8,128)(2,1)} %concatenate.3.msg_ref, bf16[128,128]{1,0:T(8,128)(2,1)} %constant.4.clone.tb_ref, bf16[256,256]{1,0:T(8,128)(2,1)} %constant.5.clone.t2_ref, ...), custom_call_target="tpu_custom_call" | custom-call | tf_op jit(solution)/shard_map/polarizability/pallas_call | solution.py:304
  54.3 1.7 %copy.12 = f32[1,128,512]{2,1,0:T(8,128)} copy(f32[1,128,512]{2,1,0:T(8,128)} %bitcast.8) | data formatting | bytes 524288
  (1 shorter events, 0.0 us)
Async XLA Ops:
  0.0 1.3 %copy-start = (bf16[1,2048]{1,0:T(2,128)(2,1)S(1)}, bf16[1,2048]{1,0:T(2,128)(2,1)}, u32[]{:S(2)}) copy-start(bf16[1,2048]{1,0:T(2,128)(2,1)} %param.10) | copy-start | bytes 12292

commit v4 on v3

--- a/solution.py
+++ b/solution.py
@@ -191,7 +191,7 @@
         )
 
     def step3(t):
-        dest = lax.rem(mz + 1 + t // 2, groups) * 4 + my * 2 + mx
+        dest = xor(mz, groups - 1 - t // 2) * 4 + my * 2 + mx
         return remote(send3.at[t], got3.at[t], s3.at[t], r3.at[t], dest)
 
     def both(t):
@@ -207,7 +207,7 @@
         @pl.when(i < chunks)
         def _():
             t = i
-            z = lax.rem(mz + 1 + t // 2, groups)
+            z = xor(mz, groups - 1 - t // 2)
             col = pl.multiple_of(lax.rem(t, 2) * half, half)
             acc = lax.dot_general(
                 moved[pl.ds(pl.multiple_of(z * 4 * rows, 4 * rows), 4 * rows), :],

time: 56.2 us -> 57.2 us (1.018)
  Pallas kernels: 52.3 us -> 53.4 us
    pallas_call x1, Pallas kernels: 52.3 us -> 53.4 us  [shards(): pl.pallas_call(functools.partial(kernel, ka_size, n, scale), out_shape=ja...]
where the time goes in v4:
time: 57.2 us; the launch traced here: 57 us
  Pallas kernels  53.4 us (93%)
  local copies, waits for them, and re-layouts  2.27 us (4%)
  between operations  1.34 us (2%)
    pallas_call x1, Pallas kernels, shards(): pl.pallas_call(functools.partial(kernel, ka_size, n, scale), out_shape=ja...  53.4 us
    unnamed x3, local copies, waits for them, and re-layouts  1.68 us

profile of v4, /device:TPU:0, one launch (start us, length us, event | category | flops | bytes accessed | tf_op | source)
XLA Modules:
  0.0 57.0 jit_solution(8543820392611515054)
XLA Ops:
  0.0 0.0 copy-start
  1.3 0.0 copy-done
  1.4 0.6 %concatenate.3.msg_ref = bf16[24,128]{1,0:T(8,128)(2,1)} pad(bf16[16,128]{1,0:T(8,128)(2,1)S(1)} %bitcast.10, bf16[]{:T(256)} %bitcast.6), padding=0_8x0_0 | pad | bytes 10242 | tf_op jit(solution)/shard_map/concatenate | solution.py:294
  2.0 53.4 %polarizability.1 = f32[128,512]{1,0:T(8,128)} custom-call(s32[16]{0:T(128)} %bitcast.11, s32[1]{0:T(128)} %bitcast.7.count_ref, f32[1,128]{1,0:T(1,128)} %ec_ref.1, bf16[24,128]{1,0:T(8,128)(2,1)} %concatenate.3.msg_ref, bf16[128,128]{1,0:T(8,128)(2,1)} %constant.4.clone.tb_ref, bf16[256,256]{1,0:T(8,128)(2,1)} %constant.5.clone.t2_ref, ...), custom_call_target="tpu_custom_call" | custom-call | tf_op jit(solution)/shard_map/polarizability/pallas_call | solution.py:304
  55.4 1.7 %copy.12 = f32[1,128,512]{2,1,0:T(8,128)} copy(f32[1,128,512]{2,1,0:T(8,128)} %bitcast.8) | data formatting | bytes 524288
  (1 shorter events, 0.0 us)
Async XLA Ops:
  0.0 1.3 %copy-start = (bf16[1,2048]{1,0:T(2,128)(2,1)S(1)}, bf16[1,2048]{1,0:T(2,128)(2,1)}, u32[]{:S(2)}) copy-start(bf16[1,2048]{1,0:T(2,128)(2,1)} %param.10) | copy-start | bytes 12292
